TPU v7x, 32 devices: a whole 2x2x4 slice. The times are simulated.
32 devices in a mesh: dp: 16 (over z, x, core), tensor: 2 (over y).
Axes of the slice: x: 2, y: 2, z: 4, core: 2. Of those that a mesh axis runs over, the one named last changes fastest.
Arguments:
- features: bfloat16 [512, 16, 4096], P('tensor', 'dp'), may hold values from -6 to 6
- cotangent: bfloat16 [512, 16, 4096], P('tensor', 'dp'), may hold values from -6 to 6
- embedding: bfloat16 [16, 2048], P('dp'), may hold values from -6 to 6
- context: bfloat16 [16, 260, 2048], P('dp'), may hold values from -6 to 6
- lengths: int32 [16], P('dp'), may hold values from 5 to 256, as said below
- norm1_gain: float32 [512], P('tensor'), may hold values from 0.25 to 1.75
- norm1_bias: float32 [512], P('tensor'), may hold values from -2 to 2
- conv1_weight: bfloat16 [512, 4608], P('tensor'), may hold values from -0.09375 to 0.09375
- conv1_bias: float32 [512], P('tensor'), may hold values from -2 to 2
- emb_weight: bfloat16 [2, 2048, 512], P(None, None, 'tensor'), may hold values from -0.125 to 0.125
- emb_bias: float32 [2, 512], P(None, 'tensor'), may hold values from -2 to 2
- norm2_gain: float32 [512], P('tensor'), may hold values from 0.25 to 1.75
- norm2_bias: float32 [512], P('tensor'), may hold values from -2 to 2
- conv2_weight: bfloat16 [512, 4608], P('tensor'), may hold values from -0.09375 to 0.09375
- conv2_bias: float32 [512], P('tensor'), may hold values from -2 to 2
- norm3_gain: float32 [512], P('tensor'), may hold values from 0.25 to 1.75
- norm3_bias: float32 [512], P('tensor'), may hold values from -2 to 2
- qkv_weight: bfloat16 [3, 512, 512], P(None, 'tensor'), may hold values from -0.25 to 0.25
- qkv_bias: float32 [3, 512], P(None, 'tensor'), may hold values from -2 to 2
- context_weight: bfloat16 [2, 512, 2048], P(None, 'tensor'), may hold values from -0.125 to 0.125
- context_bias: float32 [2, 512], P(None, 'tensor'), may hold values from -2 to 2
- out_weight: bfloat16 [512, 512], P('tensor'), may hold values from -2 to 2
- out_bias: float32 [512], P('tensor'), may hold values from -2 to 2
Outputs:
- output: bfloat16 [512, 16, 4096], P('tensor', 'dp')
- input_grad: float32 [512, 16, 4096], P('tensor', 'dp')
- norm1_gain_grad: float32 [512], P('tensor')
- norm1_bias_grad: float32 [512], P('tensor')
- conv1_weight_grad: float32 [512, 4608], P('tensor')
- conv1_bias_grad: float32 [512], P('tensor')
- emb_weight_grad: float32 [2, 2048, 512], P(None, None, 'tensor')
- emb_bias_grad: float32 [2, 512], P(None, 'tensor')
- norm2_gain_grad: float32 [512], P('tensor')
- norm2_bias_grad: float32 [512], P('tensor')
- conv2_weight_grad: float32 [512, 4608], P('tensor')
- conv2_bias_grad: float32 [512], P('tensor')
- norm3_gain_grad: float32 [512], P('tensor')
- norm3_bias_grad: float32 [512], P('tensor')
- qkv_weight_grad: float32 [3, 512, 512], P(None, 'tensor')
- qkv_bias_grad: float32 [3, 512], P(None, 'tensor')
- context_weight_grad: float32 [2, 512, 2048], P(None, 'tensor')
- context_bias_grad: float32 [2, 512], P(None, 'tensor')
- out_weight_grad: float32 [512, 512], P('tensor')
- out_bias_grad: float32 [512], P('tensor')
Inputs may be any that keep to these rules, and one draw needn't show every extreme that they name: `lengths`: each image's number of real text tokens; some image has 256.
All inputs are finite; a program needn't handle non-finite values.
Results may differ from a plain program's by a relative error of at most 0.025.
Values may be sent and summed in bfloat16 or wider, within the bound.
No kernel may reach another device: no remote copies, remote signals or barrier semaphores. Data moves between devices by JAX's collectives and lax.ppermute only.
A program may use at most 384 MiB of HBM per device.

v0:
```python
import jax
import jax.numpy as jnp
from jax import lax
from jax.sharding import PartitionSpec as P

C = 512
HEAD_DIM = 64
GROUPS = 32
SIDE = 64
HW = 4096
CTX = 260
EPSILON = 1e-05
NEG_FILL = -1e30


def group_norm(values, gain_vec, bias_vec):
    channels, images, pixels = values.shape
    per_group = C // GROUPS
    grouped = values.reshape(channels // per_group, per_group, images, pixels)
    group_mean = jnp.mean(grouped, axis=(1, 3), keepdims=True)
    group_var = jnp.mean(jnp.square(grouped - group_mean), axis=(1, 3), keepdims=True)
    normal_vals = ((grouped - group_mean) * lax.rsqrt(group_var + EPSILON)).reshape(values.shape)
    return normal_vals * gain_vec[:, None, None] + bias_vec[:, None, None]


def shifted(values, kernel_tap):
    row_off, col_off = (kernel_tap // 3, kernel_tap % 3)
    channels, images, pixels = values.shape
    padded = jnp.pad(values.reshape(channels, images, SIDE, SIDE), ((0, 0), (0, 0), (1, 1), (1, 1)))
    return padded[:, :, row_off : row_off + SIDE, col_off : col_off + SIDE].reshape(
        channels, images, pixels
    )


def convolve(full_act, weight, bias_vec):
    kernel = weight.reshape(weight.shape[0], 9, C)
    result = (
        jnp.zeros((weight.shape[0],) + full_act.shape[1:], jnp.float32) + bias_vec[:, None, None]
    )
    for kernel_tap in range(9):
        result = result + jnp.einsum(
            "oc,cip->oip",
            kernel[:, kernel_tap],
            shifted(full_act, kernel_tap),
            preferred_element_type=jnp.float32,
        )
    return result


def kernel_grad(grad_low, full_act):
    pieces = [
        jnp.einsum(
            "oip,cip->oc",
            grad_low,
            shifted(full_act, kernel_tap),
            preferred_element_type=jnp.float32,
        )
        for kernel_tap in range(9)
    ]
    return jnp.stack(pieces, axis=1).reshape(grad_low.shape[0], 9 * C)


def conv_input_grad(grad_low, weight):
    channels = grad_low.shape[0]
    kernel = weight.reshape(channels, 9, C)
    moved_grads = [shifted(grad_low, 8 - kernel_tap) for kernel_tap in range(9)]
    result = jnp.zeros((lax.axis_size("tensor") * channels,) + grad_low.shape[1:], jnp.float32)
    for kernel_tap in range(9):
        cols_part = kernel[:, kernel_tap]
        result = result + jnp.einsum(
            "oc,oip->cip", cols_part, moved_grads[kernel_tap], preferred_element_type=jnp.float32
        )
    return lax.psum_scatter(
        result.astype(jnp.bfloat16), "tensor", scatter_dimension=0, tiled=True
    ).astype(jnp.float32)


def to_heads(values):
    channels, images, length_n = values.shape
    return (
        values.reshape(channels // HEAD_DIM, HEAD_DIM, images, length_n)
        .transpose(2, 0, 1, 3)
        .reshape(-1, HEAD_DIM, length_n)
    )


def from_heads(values, images):
    groups_n, head_dims, length_n = values.shape
    heads_here = groups_n // images
    return (
        values.reshape(images, heads_here, head_dims, length_n)
        .transpose(1, 2, 0, 3)
        .reshape(heads_here * head_dims, images, length_n)
    )


def masked_scores(q_block, key_rows, key_valid):
    scores = jnp.einsum(
        "gdi,gdj->gij", q_block, key_rows, preferred_element_type=jnp.float32
    ) * HEAD_DIM ** (-0.5)
    return jnp.where(key_valid[:, None, :], scores, NEG_FILL)


def attend_forward(queries, key_rows, value_rows, key_valid):
    groups_n = queries.shape[0]
    block_len = min(512, HW)
    blocks_q = queries.reshape(groups_n, HEAD_DIM, HW // block_len, block_len).transpose(2, 0, 1, 3)

    def one_block(q_block):
        scores = masked_scores(q_block, key_rows, key_valid)
        row_top = jnp.max(scores, axis=-1, keepdims=True)
        raised = jnp.exp(scores - row_top)
        row_total = jnp.sum(raised, axis=-1, keepdims=True)
        probs_low = (raised / row_total).astype(jnp.bfloat16)
        mixed_out = jnp.einsum(
            "gdj,gij->gdi", value_rows, probs_low, preferred_element_type=jnp.float32
        )
        return (mixed_out.astype(jnp.bfloat16), row_top, row_total)

    mixed_out, row_top, row_total = lax.map(one_block, blocks_q)
    merged = mixed_out.transpose(1, 2, 0, 3).reshape(groups_n, HEAD_DIM, HW)
    return (merged, row_top, row_total)


def attend_backward(queries, key_rows, value_rows, key_valid, grad_mixed, row_top, row_total):
    groups_n = queries.shape[0]
    block_len = min(512, HW)
    count_b = HW // block_len
    blocks_q = queries.reshape(groups_n, HEAD_DIM, count_b, block_len).transpose(2, 0, 1, 3)
    blocks_g = grad_mixed.reshape(groups_n, HEAD_DIM, count_b, block_len).transpose(2, 0, 1, 3)
    scale_val = HEAD_DIM ** (-0.5)

    def one_block(carried, packed):
        key_acc, value_acc = carried
        q_block, g_block, block_top, block_total = packed
        scores = masked_scores(q_block, key_rows, key_valid)
        prob_f32 = jnp.exp(scores - block_top) / block_total
        probs_low = prob_f32.astype(jnp.bfloat16)
        value_acc = value_acc + jnp.einsum(
            "gdi,gij->gdj", g_block, probs_low, preferred_element_type=jnp.float32
        )
        grad_probs = jnp.einsum(
            "gdi,gdj->gij", g_block, value_rows, preferred_element_type=jnp.float32
        )
        delta_row = jnp.sum(prob_f32 * grad_probs, axis=-1, keepdims=True)
        grad_scores = (prob_f32 * (grad_probs - delta_row)).astype(jnp.bfloat16)
        grad_query = (
            jnp.einsum("gij,gdj->gdi", grad_scores, key_rows, preferred_element_type=jnp.float32)
            * scale_val
        )
        key_acc = (
            key_acc
            + jnp.einsum("gij,gdi->gdj", grad_scores, q_block, preferred_element_type=jnp.float32)
            * scale_val
        )
        return ((key_acc, value_acc), grad_query)

    zero_acc = jnp.zeros(key_rows.shape, jnp.float32)
    (key_grad, value_grad), query_grad = lax.scan(
        one_block, (zero_acc, zero_acc), (blocks_q, blocks_g, row_top, row_total)
    )
    query_grad = query_grad.transpose(1, 2, 0, 3).reshape(groups_n, HEAD_DIM, HW)
    return (query_grad, key_grad, value_grad)


def first_section(values, gain_vec, bias_vec):
    return jax.nn.silu(group_norm(values, gain_vec, bias_vec))


def second_section(values, gain_vec, bias_vec, modulation):
    normal_vals = group_norm(values, gain_vec, bias_vec)
    return jax.nn.silu(normal_vals * (1.0 + modulation[0][:, :, None]) + modulation[1][:, :, None])


def local(
    features,
    cotangent,
    embedding,
    context,
    lengths,
    norm1_gain,
    norm1_bias,
    conv1_weight,
    conv1_bias,
    emb_weight,
    emb_bias,
    norm2_gain,
    norm2_bias,
    conv2_weight,
    conv2_bias,
    norm3_gain,
    norm3_bias,
    qkv_weight,
    qkv_bias,
    context_weight,
    context_bias,
    out_weight,
    out_bias,
):
    channels, images, pixels = features.shape
    feat_f32 = features.astype(jnp.float32)
    act_one = first_section(feat_f32, norm1_gain, norm1_bias).astype(jnp.bfloat16)
    full_one = lax.all_gather(act_one, "tensor", axis=0, tiled=True)
    conv_one = convolve(full_one, conv1_weight, conv1_bias)
    emb_act = jax.nn.silu(embedding.astype(jnp.float32)).astype(jnp.bfloat16)
    scale_shift = (
        jnp.einsum("ie,teo->toi", emb_act, emb_weight, preferred_element_type=jnp.float32)
        + emb_bias[:, :, None]
    )
    act_two = second_section(conv_one, norm2_gain, norm2_bias, scale_shift).astype(jnp.bfloat16)
    full_two = lax.all_gather(act_two, "tensor", axis=0, tiled=True)
    hidden = feat_f32 + convolve(full_two, conv2_weight, conv2_bias)
    normed = group_norm(hidden, norm3_gain, norm3_bias).astype(jnp.bfloat16)
    full_three = lax.all_gather(normed, "tensor", axis=0, tiled=True)
    qkv_low = (
        jnp.einsum("toc,cip->toip", qkv_weight, full_three, preferred_element_type=jnp.float32)
        + qkv_bias[:, :, None, None]
    ).astype(jnp.bfloat16)
    ctx_low = (
        jnp.einsum("toe,ine->toin", context_weight, context, preferred_element_type=jnp.float32)
        + context_bias[:, :, None, None]
    ).astype(jnp.bfloat16)
    queries = to_heads(qkv_low[0])
    key_rows = jnp.concatenate([to_heads(qkv_low[1]), to_heads(ctx_low[0])], axis=2)
    value_rows = jnp.concatenate([to_heads(qkv_low[2]), to_heads(ctx_low[1])], axis=2)
    key_limit = HW + 4 + lengths
    key_valid = jnp.repeat(
        jnp.arange(HW + CTX, dtype=jnp.int32)[None, :] < key_limit[:, None],
        channels // HEAD_DIM,
        axis=0,
    )
    heads_mixed, row_top, row_total = attend_forward(queries, key_rows, value_rows, key_valid)
    heads_out = from_heads(heads_mixed, images)
    full_heads = lax.all_gather(heads_out, "tensor", axis=0, tiled=True)
    output = (
        hidden
        + jnp.einsum("oc,cip->oip", out_weight, full_heads, preferred_element_type=jnp.float32)
        + out_bias[:, None, None]
    ).astype(jnp.bfloat16)
    grad_top = cotangent.astype(jnp.float32)
    out_weight_grad = jnp.einsum(
        "oip,cip->oc", cotangent, full_heads, preferred_element_type=jnp.float32
    )
    out_bias_grad = jnp.sum(grad_top, axis=(1, 2))
    cols_part = out_weight
    grad_heads = lax.psum_scatter(
        jnp.einsum("oc,oip->cip", cols_part, cotangent, preferred_element_type=jnp.float32).astype(
            jnp.bfloat16
        ),
        "tensor",
        scatter_dimension=0,
        tiled=True,
    )
    query_grad, key_grad, value_grad = attend_backward(
        queries, key_rows, value_rows, key_valid, to_heads(grad_heads), row_top, row_total
    )
    grad_qkv = jnp.stack(
        [
            from_heads(query_grad, images),
            from_heads(key_grad[:, :, :HW], images),
            from_heads(value_grad[:, :, :HW], images),
        ]
    ).astype(jnp.bfloat16)
    grad_ctx = jnp.stack(
        [from_heads(key_grad[:, :, HW:], images), from_heads(value_grad[:, :, HW:], images)]
    ).astype(jnp.bfloat16)
    qkv_weight_grad = jnp.einsum(
        "toip,cip->toc", grad_qkv, full_three, preferred_element_type=jnp.float32
    )
    qkv_bias_grad = jnp.sum(grad_qkv.astype(jnp.float32), axis=(2, 3))
    context_weight_grad = jnp.einsum(
        "toin,ine->toe", grad_ctx, context, preferred_element_type=jnp.float32
    )
    context_bias_grad = jnp.sum(grad_ctx.astype(jnp.float32), axis=(2, 3))
    cols_part = qkv_weight
    grad_normed = lax.psum_scatter(
        jnp.einsum("toc,toip->cip", cols_part, grad_qkv, preferred_element_type=jnp.float32).astype(
            jnp.bfloat16
        ),
        "tensor",
        scatter_dimension=0,
        tiled=True,
    ).astype(jnp.float32)
    unused_three, pull_three = jax.vjp(group_norm, hidden, norm3_gain, norm3_bias)
    grad_branch, norm3_gain_grad, norm3_bias_grad = pull_three(grad_normed)
    grad_hidden = grad_top + grad_branch
    attention_grads = (
        lax.psum(out_weight_grad.astype(jnp.bfloat16), "dp").astype(jnp.float32),
        lax.psum(out_bias_grad.astype(jnp.bfloat16), "dp").astype(jnp.float32),
        lax.psum(qkv_weight_grad.astype(jnp.bfloat16), "dp").astype(jnp.float32),
        lax.psum(qkv_bias_grad.astype(jnp.bfloat16), "dp").astype(jnp.float32),
        lax.psum(context_weight_grad.astype(jnp.bfloat16), "dp").astype(jnp.float32),
        lax.psum(context_bias_grad.astype(jnp.bfloat16), "dp").astype(jnp.float32),
        lax.psum(norm3_gain_grad.astype(jnp.bfloat16), "dp").astype(jnp.float32),
        lax.psum(norm3_bias_grad.astype(jnp.bfloat16), "dp").astype(jnp.float32),
    )
    grad_conv_two = grad_hidden.astype(jnp.bfloat16)
    conv2_bias_grad = jnp.sum(grad_conv_two.astype(jnp.float32), axis=(1, 2))
    conv2_weight_grad = kernel_grad(grad_conv_two, full_two)
    grad_act_two = conv_input_grad(grad_conv_two, conv2_weight)
    unused_two, pull_two = jax.vjp(second_section, conv_one, norm2_gain, norm2_bias, scale_shift)
    grad_conv_one, norm2_gain_grad, norm2_bias_grad, grad_modulation = pull_two(grad_act_two)
    grad_mod_low = grad_modulation.astype(jnp.bfloat16)
    emb_weight_grad = jnp.einsum(
        "ie,toi->teo", emb_act, grad_mod_low, preferred_element_type=jnp.float32
    )
    emb_bias_grad = jnp.sum(grad_mod_low.astype(jnp.float32), axis=2)
    grad_conv_low = grad_conv_one.astype(jnp.bfloat16)
    conv1_bias_grad = jnp.sum(grad_conv_low.astype(jnp.float32), axis=(1, 2))
    conv1_weight_grad = kernel_grad(grad_conv_low, full_one)
    grad_act_one = conv_input_grad(grad_conv_low, conv1_weight)
    unused_one, pull_one = jax.vjp(first_section, feat_f32, norm1_gain, norm1_bias)
    grad_feat, norm1_gain_grad, norm1_bias_grad = pull_one(grad_act_one)
    input_grad = grad_hidden + grad_feat
    residual_grads = (
        lax.psum(norm1_gain_grad.astype(jnp.bfloat16), "dp").astype(jnp.float32),
        lax.psum(norm1_bias_grad.astype(jnp.bfloat16), "dp").astype(jnp.float32),
        lax.psum(conv1_weight_grad.astype(jnp.bfloat16), "dp").astype(jnp.float32),
        lax.psum(conv1_bias_grad.astype(jnp.bfloat16), "dp").astype(jnp.float32),
        lax.psum(emb_weight_grad.astype(jnp.bfloat16), "dp").astype(jnp.float32),
        lax.psum(emb_bias_grad.astype(jnp.bfloat16), "dp").astype(jnp.float32),
        lax.psum(norm2_gain_grad.astype(jnp.bfloat16), "dp").astype(jnp.float32),
        lax.psum(norm2_bias_grad.astype(jnp.bfloat16), "dp").astype(jnp.float32),
        lax.psum(conv2_weight_grad.astype(jnp.bfloat16), "dp").astype(jnp.float32),
        lax.psum(conv2_bias_grad.astype(jnp.bfloat16), "dp").astype(jnp.float32),
    )
    return (
        output,
        input_grad,
        residual_grads[0],
        residual_grads[1],
        residual_grads[2],
        residual_grads[3],
        residual_grads[4],
        residual_grads[5],
        residual_grads[6],
        residual_grads[7],
        residual_grads[8],
        residual_grads[9],
        attention_grads[6],
        attention_grads[7],
        attention_grads[2],
        attention_grads[3],
        attention_grads[4],
        attention_grads[5],
        attention_grads[0],
        attention_grads[1],
    )


def solution(mesh):
    placed = (
        P("tensor", "dp", None),
        P("tensor", "dp", None),
        P("dp", None),
        P("dp", None, None),
        P("dp"),
        P("tensor"),
        P("tensor"),
        P("tensor", None),
        P("tensor"),
        P(None, None, "tensor"),
        P(None, "tensor"),
        P("tensor"),
        P("tensor"),
        P("tensor", None),
        P("tensor"),
        P("tensor"),
        P("tensor"),
        P(None, "tensor", None),
        P(None, "tensor"),
        P(None, "tensor", None),
        P(None, "tensor"),
        P("tensor", None),
        P("tensor"),
    )
    return jax.shard_map(
        local,
        mesh=mesh,
        in_specs=placed,
        out_specs=(
            P("tensor", "dp", None),
            P("tensor", "dp", None),
            P("tensor"),
            P("tensor"),
            P("tensor", None),
            P("tensor"),
            P(None, None, "tensor"),
            P(None, "tensor"),
            P("tensor"),
            P("tensor"),
            P("tensor", None),
            P("tensor"),
            P("tensor"),
            P("tensor"),
            P(None, "tensor", None),
            P(None, "tensor"),
            P(None, "tensor", None),
            P(None, "tensor"),
            P("tensor", None),
            P("tensor"),
        ),
        check_vma=False,
    )
```

profile of v0, /device:TPU:0, one launch (start us, length us, event | category | flops | bytes accessed | tf_op | source)
XLA Modules:
  0.0 2261.5 jit_solution(17377600485982242379)
XLA Ops:
  27.8 53.2 %all-gather.6.cloned.1.call-done = bf16[512,1,4096]{0,2,1:T(8,128)(2,1)} async-done(((bf16[256,1,4096]{0,2,1:T(8,128)(2,1)}), bf16[512,1,4096]{0,2,1:T(8,128)(2,1)}) %all-gather.6.cloned.1.call-update) | async-done | bytes 4194320 | tf_op jit(solution)/shard_map/all_gather | solution.py:203
  81.0 22.1 pad_slice_fusion.8
  147.0 47.4 %all-gather.12.cloned.1.call-done = bf16[512,4096]{0,1:T(8,128)(2,1)} async-done(((bf16[256,4096]{0,1:T(8,128)(2,1)}), bf16[512,4096]{0,1:T(8,128)(2,1)}) %all-gather.12.cloned.1.call-update) | async-done | bytes 4194320 | tf_op jit(solution)/shard_map/all_gather | solution.py:211
  194.5 21.5 pad_slice_fusion
  257.5 51.8 %all-gather.8.cloned.1.call-done = bf16[512,1,4096]{0,2,1:T(8,128)(2,1)} async-done(((bf16[256,1,4096]{0,2,1:T(8,128)(2,1)}), bf16[512,1,4096]{0,2,1:T(8,128)(2,1)}) %all-gather.8.cloned.1.call-update) | async-done | bytes 4194320 | tf_op jit(solution)/shard_map/all_gather | solution.py:214
  322.8 393.9 %while.30 = (s32[]{:T(128)}, bf16[8,4,64,512]{3,2,1,0:T(8,128)(2,1)}, f32[8,4,512,1]{2,1,3,0:T(4,128)S(1)}, f32[8,4,512,1]{2,1,3,0:T(4,128)S(1)}, bf16[8,4,64,51...) while((s32[]{:T(128)}, ...), condition=%wide.region_15.16_spmd.clone, body=%wide.region_12.15_spmd.clone.sunk | while | flops 2390978560 | bytes 121079936 | solution.py:120
  322.8 16.9 fusion.444
  372.0 16.9 fusion.444
  421.3 16.9 fusion.444
  519.7 16.9 fusion.444
  716.7 922.0 %while.31 = (s32[]{:T(128)}, f32[4,64,4356]{2,1,0:T(8,128)}, f32[4,64,4356]{2,1,0:T(8,128)}, bf16[8,4,64,512]{3,2,1,0:T(8,128)(2,1)}, bf16[8,4,64,512]{3,2,1,0:T...) while((s32[]{:T(128)}, f32[4,64,4356]{2,1,0:T(8,128)}, ...), condition=%wide.region_19.20_spmd.clone, body=%wide.region_17.19_spmd.clone.sunk | while | flops 5804411904 | bytes 302971552 | solution.py:159
  716.8 18.3 fusion.456
  735.2 30.3 %multiply_reduce_fusion.7 = (f32[4,512]{1,0:T(4,128)S(1)}, f32[4,512,4356]{1,2,0:T(8,128)}) fusion(f32[4,512,4356]{1,2,0:T(8,128)} %fusion.456, f32[4,512]{1,0:T(4,128)S(1)} %get-tuple-element.508, f32[4,512]{1,0:T(4,128)S(1)} %get-tuple-element.509, bf16[4,64,4356]{2,1,0:T(8,128)(2,1)} %get-tuple-element.570, ...), kind=kOutput, calls=%fused_computation.20.clone.1 | convolution fusion | flops 1195423744 | bytes 73890816 | tf_op jit(solution)/shard_map/while/body/eval_jaxpr/gdi,gdj->gij/dot_general | solution.py:98
  765.5 29.7 %multiply_convert_fusion.4 = bf16[4,512,4356]{1,2,0:T(8,128)(2,1)} fusion(f32[4,512,4356]{1,2,0:T(8,128)} %get-tuple-element.510, f32[4,512,4356]{1,2,0:T(8,128)} %fusion.456, f32[4,512]{1,0:T(4,128)S(1)} %get-tuple-element.511), kind=kLoop, calls=%fused_computation.19.clone.1 | loop fusion | flops 26763264 | bytes 89219072 | tf_op jit(solution)/shard_map/while/body/eval_jaxpr/convert_element_type | solution.py:146
  829.5 18.3 fusion.456
  847.9 30.3 %multiply_reduce_fusion.7 = (f32[4,512]{1,0:T(4,128)S(1)}, f32[4,512,4356]{1,2,0:T(8,128)}) fusion(f32[4,512,4356]{1,2,0:T(8,128)} %fusion.456, f32[4,512]{1,0:T(4,128)S(1)} %get-tuple-element.508, f32[4,512]{1,0:T(4,128)S(1)} %get-tuple-element.509, bf16[4,64,4356]{2,1,0:T(8,128)(2,1)} %get-tuple-element.570, ...), kind=kOutput, calls=%fused_computation.20.clone.1 | convolution fusion | flops 1195423744 | bytes 73890816 | tf_op jit(solution)/shard_map/while/body/eval_jaxpr/gdi,gdj->gij/dot_general | solution.py:98
  878.1 29.7 %multiply_convert_fusion.4 = bf16[4,512,4356]{1,2,0:T(8,128)(2,1)} fusion(f32[4,512,4356]{1,2,0:T(8,128)} %get-tuple-element.510, f32[4,512,4356]{1,2,0:T(8,128)} %fusion.456, f32[4,512]{1,0:T(4,128)S(1)} %get-tuple-element.511), kind=kLoop, calls=%fused_computation.19.clone.1 | loop fusion | flops 26763264 | bytes 89219072 | tf_op jit(solution)/shard_map/while/body/eval_jaxpr/convert_element_type | solution.py:146
  928.1 17.0 fusion.458
  945.1 18.3 fusion.456
  963.4 30.3 %multiply_reduce_fusion.7 = (f32[4,512]{1,0:T(4,128)S(1)}, f32[4,512,4356]{1,2,0:T(8,128)}) fusion(f32[4,512,4356]{1,2,0:T(8,128)} %fusion.456, f32[4,512]{1,0:T(4,128)S(1)} %get-tuple-element.508, f32[4,512]{1,0:T(4,128)S(1)} %get-tuple-element.509, bf16[4,64,4356]{2,1,0:T(8,128)(2,1)} %get-tuple-element.570, ...), kind=kOutput, calls=%fused_computation.20.clone.1 | convolution fusion | flops 1195423744 | bytes 73890816 | tf_op jit(solution)/shard_map/while/body/eval_jaxpr/gdi,gdj->gij/dot_general | solution.py:98
  993.7 29.7 %multiply_convert_fusion.4 = bf16[4,512,4356]{1,2,0:T(8,128)(2,1)} fusion(f32[4,512,4356]{1,2,0:T(8,128)} %get-tuple-element.510, f32[4,512,4356]{1,2,0:T(8,128)} %fusion.456, f32[4,512]{1,0:T(4,128)S(1)} %get-tuple-element.511), kind=kLoop, calls=%fused_computation.19.clone.1 | loop fusion | flops 26763264 | bytes 89219072 | tf_op jit(solution)/shard_map/while/body/eval_jaxpr/convert_element_type | solution.py:146
  1043.6 17.0 fusion.458
  1060.6 18.3 fusion.456
  1079.0 30.3 %multiply_reduce_fusion.7 = (f32[4,512]{1,0:T(4,128)S(1)}, f32[4,512,4356]{1,2,0:T(8,128)}) fusion(f32[4,512,4356]{1,2,0:T(8,128)} %fusion.456, f32[4,512]{1,0:T(4,128)S(1)} %get-tuple-element.508, f32[4,512]{1,0:T(4,128)S(1)} %get-tuple-element.509, bf16[4,64,4356]{2,1,0:T(8,128)(2,1)} %get-tuple-element.570, ...), kind=kOutput, calls=%fused_computation.20.clone.1 | convolution fusion | flops 1195423744 | bytes 73890816 | tf_op jit(solution)/shard_map/while/body/eval_jaxpr/gdi,gdj->gij/dot_general | solution.py:98
  1109.2 29.7 %multiply_convert_fusion.4 = bf16[4,512,4356]{1,2,0:T(8,128)(2,1)} fusion(f32[4,512,4356]{1,2,0:T(8,128)} %get-tuple-element.510, f32[4,512,4356]{1,2,0:T(8,128)} %fusion.456, f32[4,512]{1,0:T(4,128)S(1)} %get-tuple-element.511), kind=kLoop, calls=%fused_computation.19.clone.1 | loop fusion | flops 26763264 | bytes 89219072 | tf_op jit(solution)/shard_map/while/body/eval_jaxpr/convert_element_type | solution.py:146
  1159.2 17.0 fusion.458
  1176.2 18.3 fusion.456
  1194.5 30.3 %multiply_reduce_fusion.7 = (f32[4,512]{1,0:T(4,128)S(1)}, f32[4,512,4356]{1,2,0:T(8,128)}) fusion(f32[4,512,4356]{1,2,0:T(8,128)} %fusion.456, f32[4,512]{1,0:T(4,128)S(1)} %get-tuple-element.508, f32[4,512]{1,0:T(4,128)S(1)} %get-tuple-element.509, bf16[4,64,4356]{2,1,0:T(8,128)(2,1)} %get-tuple-element.570, ...), kind=kOutput, calls=%fused_computation.20.clone.1 | convolution fusion | flops 1195423744 | bytes 73890816 | tf_op jit(solution)/shard_map/while/body/eval_jaxpr/gdi,gdj->gij/dot_general | solution.py:98
  1224.8 29.7 %multiply_convert_fusion.4 = bf16[4,512,4356]{1,2,0:T(8,128)(2,1)} fusion(f32[4,512,4356]{1,2,0:T(8,128)} %get-tuple-element.510, f32[4,512,4356]{1,2,0:T(8,128)} %fusion.456, f32[4,512]{1,0:T(4,128)S(1)} %get-tuple-element.511), kind=kLoop, calls=%fused_computation.19.clone.1 | loop fusion | flops 26763264 | bytes 89219072 | tf_op jit(solution)/shard_map/while/body/eval_jaxpr/convert_element_type | solution.py:146
  1274.7 17.0 fusion.458
  1291.7 18.3 fusion.456
  1310.1 30.3 %multiply_reduce_fusion.7 = (f32[4,512]{1,0:T(4,128)S(1)}, f32[4,512,4356]{1,2,0:T(8,128)}) fusion(f32[4,512,4356]{1,2,0:T(8,128)} %fusion.456, f32[4,512]{1,0:T(4,128)S(1)} %get-tuple-element.508, f32[4,512]{1,0:T(4,128)S(1)} %get-tuple-element.509, bf16[4,64,4356]{2,1,0:T(8,128)(2,1)} %get-tuple-element.570, ...), kind=kOutput, calls=%fused_computation.20.clone.1 | convolution fusion | flops 1195423744 | bytes 73890816 | tf_op jit(solution)/shard_map/while/body/eval_jaxpr/gdi,gdj->gij/dot_general | solution.py:98
  1340.3 29.7 %multiply_convert_fusion.4 = bf16[4,512,4356]{1,2,0:T(8,128)(2,1)} fusion(f32[4,512,4356]{1,2,0:T(8,128)} %get-tuple-element.510, f32[4,512,4356]{1,2,0:T(8,128)} %fusion.456, f32[4,512]{1,0:T(4,128)S(1)} %get-tuple-element.511), kind=kLoop, calls=%fused_computation.19.clone.1 | loop fusion | flops 26763264 | bytes 89219072 | tf_op jit(solution)/shard_map/while/body/eval_jaxpr/convert_element_type | solution.py:146
  1390.2 17.0 fusion.458
  1407.2 18.3 fusion.456
  1425.6 30.3 %multiply_reduce_fusion.7 = (f32[4,512]{1,0:T(4,128)S(1)}, f32[4,512,4356]{1,2,0:T(8,128)}) fusion(f32[4,512,4356]{1,2,0:T(8,128)} %fusion.456, f32[4,512]{1,0:T(4,128)S(1)} %get-tuple-element.508, f32[4,512]{1,0:T(4,128)S(1)} %get-tuple-element.509, bf16[4,64,4356]{2,1,0:T(8,128)(2,1)} %get-tuple-element.570, ...), kind=kOutput, calls=%fused_computation.20.clone.1 | convolution fusion | flops 1195423744 | bytes 73890816 | tf_op jit(solution)/shard_map/while/body/eval_jaxpr/gdi,gdj->gij/dot_general | solution.py:98
  1455.9 29.7 %multiply_convert_fusion.4 = bf16[4,512,4356]{1,2,0:T(8,128)(2,1)} fusion(f32[4,512,4356]{1,2,0:T(8,128)} %get-tuple-element.510, f32[4,512,4356]{1,2,0:T(8,128)} %fusion.456, f32[4,512]{1,0:T(4,128)S(1)} %get-tuple-element.511), kind=kLoop, calls=%fused_computation.19.clone.1 | loop fusion | flops 26763264 | bytes 89219072 | tf_op jit(solution)/shard_map/while/body/eval_jaxpr/convert_element_type | solution.py:146
  1505.8 17.0 fusion.458
  1522.8 18.3 fusion.456
  1541.1 30.3 %multiply_reduce_fusion.7 = (f32[4,512]{1,0:T(4,128)S(1)}, f32[4,512,4356]{1,2,0:T(8,128)}) fusion(f32[4,512,4356]{1,2,0:T(8,128)} %fusion.456, f32[4,512]{1,0:T(4,128)S(1)} %get-tuple-element.508, f32[4,512]{1,0:T(4,128)S(1)} %get-tuple-element.509, bf16[4,64,4356]{2,1,0:T(8,128)(2,1)} %get-tuple-element.570, ...), kind=kOutput, calls=%fused_computation.20.clone.1 | convolution fusion | flops 1195423744 | bytes 73890816 | tf_op jit(solution)/shard_map/while/body/eval_jaxpr/gdi,gdj->gij/dot_general | solution.py:98
  1571.4 29.7 %multiply_convert_fusion.4 = bf16[4,512,4356]{1,2,0:T(8,128)(2,1)} fusion(f32[4,512,4356]{1,2,0:T(8,128)} %get-tuple-element.510, f32[4,512,4356]{1,2,0:T(8,128)} %fusion.456, f32[4,512]{1,0:T(4,128)S(1)} %get-tuple-element.511), kind=kLoop, calls=%fused_computation.19.clone.1 | loop fusion | flops 26763264 | bytes 89219072 | tf_op jit(solution)/shard_map/while/body/eval_jaxpr/convert_element_type | solution.py:146
  1621.3 17.0 fusion.458
  1683.3 45.2 %reduce-scatter.7.cloned.1.call-done = bf16[256,1,4096]{0,2,1:T(8,128)(2,1)} async-done(((bf16[512,1,4096]{0,2,1:T(8,128)(2,1)}), bf16[256,1,4096]{0,2,1:T(8,128)(2,1)}) %reduce-scatter.7.cloned.1.call-update) | async-done | bytes 2097168 | tf_op jit(solution)/shard_map/reduce_scatter | solution.py:276
  1789.2 24.4 %fusion.43 = bf16[512,1,4096]{0,2,1:T(8,128)(2,1)} fusion(bf16[256,4096]{0,1:T(8,128)(2,1)} %bitcast.785, f32[4096,512]{1,0:T(8,128)} %fusion.338, f32[4096,512]{1,0:T(8,128)} %fusion.337, f32[4096,512]{1,0:T(8,128)} %fusion.336, f32[4096,512]{1,0:T(8,128)} %fusion.133, f32[4096,512]{1,0:T(8,128)} %fusion.335, f32[4096,512]{1,0:T(8,128)} %fusion.334, ...), kind=kOutput, calls=%fused_computation.63 | convolution fusion | flops 1092616192 | bytes 73662464 | tf_op jit(solution)/shard_map/oc,oip->cip/dot_general | solution.py:70
  1965.8 25.2 %fusion.44 = bf16[512,1,4096]{0,2,1:T(8,128)(2,1)} fusion(bf16[256,4096]{0,1:T(8,128)(2,1)} %bitcast.784, f32[4096,512]{1,0:T(8,128)} %fusion.331, f32[4096,512]{1,0:T(8,128)} %fusion.330, f32[4096,512]{1,0:T(8,128)} %fusion.329, f32[4096,512]{1,0:T(8,128)} %fusion.113, f32[4096,512]{1,0:T(8,128)} %fusion.328, f32[4096,512]{1,0:T(8,128)} %fusion.327, ...), kind=kOutput, calls=%fused_computation.64 | convolution fusion | flops 1092616192 | bytes 73662464 | tf_op jit(solution)/shard_map/oc,oip->cip/dot_general | solution.py:70
  2012.0 119.1 %all-reduce.10.cloned.1.call-done = (bf16[256,4608]{0,1:T(8,128)(2,1)}, bf16[256,4608]{0,1:T(8,128)(2,1)}, bf16[256,512]{0,1:T(8,128)(2,1)}, bf16[2,2048,256]{2,...) async-done(((bf16[256,4608]{0,1:T(8,128)(2,1)}, bf16[256,4608]{0,1:T(8,128)(2,1)}, bf16[256,512]{0,1:T(8,128)(2,1)}, ...) | async-done | bytes 9961488 | tf_op jit(solution)/shard_map/psum | solution.py:318
  2147.7 40.5 %reduce-scatter.11.cloned.1.call-done = bf16[256,1,4096]{0,2,1:T(8,128)(2,1)} async-done(((bf16[512,1,4096]{0,2,1:T(8,128)(2,1)}), bf16[256,1,4096]{0,2,1:T(8,128)(2,1)}) %reduce-scatter.11.cloned.1.call-update) | async-done | bytes 2097168 | tf_op jit(solution)/shard_map/reduce_scatter | solution.py:73
  2194.1 34.2 %all-reduce.6 = (bf16[256]{0:T(256)(128)(2,1)S(1)}, bf16[256]{0:T(256)(128)(2,1)S(1)}, bf16[256]{0:T(256)(128)(2,1)S(1)}, bf16[2,256]{1,0:T(2,128)(2,1)S(1)}, bf...) all-reduce(bf16[256]{0:T(256)(128)(2,1)S(1)} %get-tuple-element.252, ...), channel_id=1, replica_groups=mesh['dp'=16,'tensor'=2] {'dp'}, use_global_device_ids=true, to_apply=%region_42.43 | all-reduce | flops 4096 | bytes 16384 | tf_op jit(solution)/shard_map/psum | solution.py:316
  (539 shorter events, 946.4 us)
Async XLA Ops:
  7.2 243.3 %copy-start = (bf16[2,256,2048]{2,1,0:T(8,128)(2,1)S(1)}, bf16[2,256,2048]{2,1,0:T(8,128)(2,1)}, u32[]{:S(2)}) copy-start(bf16[2,256,2048]{2,1,0:T(8,128)(2,1)} %param.46) | copy-start | bytes 6291460
  7.2 73.8 %all-gather.6.cloned.1.call-start = ((), (), s32[]{:S(2)}) async-start(), calls=%async_computation.4 | async-start | bytes 6291456 | tf_op jit(solution)/shard_map/all_gather | solution.py:203
  21.5 173.0 %all-gather.12.cloned.1.call-start = ((), (), s32[]{:S(2)}) async-start(), calls=%async_computation.11 | async-start | bytes 6291456 | tf_op jit(solution)/shard_map/all_gather | solution.py:211
  27.8 104.4 %copy-start.72 = (f32[1,256]{1,0:T(1,128)}, f32[1,256]{1,0:T(1,128)S(1)}, u32[]{:S(2)}) copy-start(f32[1,256]{1,0:T(1,128)S(1)} %get-tuple-element.370) | copy-start | bytes 3076
  27.8 104.4 %copy-start.88 = (f32[1,256]{1,0:T(1,128)}, f32[1,256]{1,0:T(1,128)S(1)}, u32[]{:S(2)}) copy-start(f32[1,256]{1,0:T(1,128)S(1)} %get-tuple-element.371) | copy-start | bytes 3076
  81.0 22.1 copy-start.97
  103.1 17.8 copy-start.17
  103.1 19.1 copy-start.15
  103.1 20.5 copy-start.13
  103.1 21.8 copy-start.11
  137.6 116.1 %reduce-scatter.5.cloned.1.call-start = ((), (), s32[]{:S(2)}) async-start(), calls=%async_computation.7 | async-start | bytes 6291456 | tf_op jit(solution)/shard_map/reduce_scatter | solution.py:246
  142.5 166.8 %all-gather.8.cloned.1.call-start = ((), (), s32[]{:S(2)}) async-start(), calls=%async_computation.5 | async-start | bytes 6291456 | tf_op jit(solution)/shard_map/all_gather | solution.py:214
  194.5 21.6 copy-start.98
  216.0 18.1 copy-start.31
  216.0 19.5 copy-start.29
  216.0 20.8 copy-start.27
  216.0 22.1 copy-start.7
  250.3 1478.1 %reduce-scatter.7.cloned.1.call-start = ((), (), s32[]{:S(2)}) async-start(), calls=%async_computation.8 | async-start | bytes 6291456 | tf_op jit(solution)/shard_map/reduce_scatter | solution.py:276
  250.5 58.8 %copy-start.110 = (bf16[3,256,512]{2,1,0:T(8,128)(2,1)S(1)}, bf16[3,256,512]{2,1,0:T(8,128)(2,1)}, u32[]{:S(2)}) copy-start(bf16[3,256,512]{2,1,0:T(8,128)(2,1)} %param.44) | copy-start | bytes 2359300
  250.5 58.8 %copy-start.112 = (f32[3,256]{1,0:T(4,128)S(1)}, f32[3,256]{1,0:T(4,128)}, u32[]{:S(2)}) copy-start(f32[3,256]{1,0:T(4,128)} %param.45) | copy-start | bytes 9220
  339.7 16.3 copy-start.6
  438.2 16.3 copy-start.6
  487.4 16.3 copy-start.6
  536.7 16.3 copy-start.6
  1674.0 154.9 %all-gather.10.cloned.1.call-start = ((), (), s32[]{:S(2)}) async-start(), calls=%async_computation.6 | async-start | bytes 6291456 | tf_op jit(solution)/shard_map/all_gather | solution.py:234
  1680.8 47.7 %copy-start.62 = (f32[256]{0:T(256)S(1)}, f32[256]{0:T(256)}, u32[]{:S(2)}) copy-start(f32[256]{0:T(256)} %copy-done.61) | copy-start | bytes 3076
  1680.8 47.7 %copy-start.75 = (f32[256]{0:T(256)S(1)}, f32[256]{0:T(256)}, u32[]{:S(2)}) copy-start(f32[256]{0:T(256)} %copy-done.74) | copy-start | bytes 3076
  1680.8 47.7 %copy-start.84 = (f32[256]{0:T(256)S(1)}, f32[256]{0:T(256)}, u32[]{:S(2)}) copy-start(f32[256]{0:T(256)} %param.42) | copy-start | bytes 3076
  1683.2 50.2 %copy-start.109 = (f32[16]{0:T(128)S(1)}, f32[16]{0:T(128)}, u32[]{:S(2)}) copy-start(f32[16]{0:T(128)} %copy-done.108) | copy-start | bytes 196
  1683.2 185.0 %reduce-scatter.9.cloned.1.call-start = ((), (), s32[]{:S(2)}) async-start(), calls=%async_computation.9 | async-start | bytes 6291456 | tf_op jit(solution)/shard_map/reduce_scatter | solution.py:73
  1813.6 317.5 %all-reduce.10.cloned.1.call-start = ((), (), s32[]{:S(2)}) async-start(), calls=%async_computation.12 | async-start | bytes 19922944 | tf_op jit(solution)/shard_map/psum | solution.py:318
  1859.0 16.7 copy-start.107
  1935.5 252.7 %reduce-scatter.11.cloned.1.call-start = ((), (), s32[]{:S(2)}) async-start(), calls=%async_computation.10 | async-start | bytes 6291456 | tf_op jit(solution)/shard_map/reduce_scatter | solution.py:73
  2142.7 45.5 %copy-start.5 = (bf16[256,1,4096]{0,2,1:T(8,128)(2,1)S(1)}, bf16[256,1,4096]{0,2,1:T(8,128)(2,1)}, u32[]{:S(2)}) copy-start(bf16[256,1,4096]{0,2,1:T(8,128)(2,1)} %copy.104) | copy-start | bytes 6291460
  2142.8 45.5 %copy-start.65 = (f32[256]{0:T(256)S(1)}, f32[256]{0:T(256)}, u32[]{:S(2)}) copy-start(f32[256]{0:T(256)} %copy-done.64) | copy-start | bytes 3076
  2142.8 45.5 %copy-start.78 = (f32[256]{0:T(256)S(1)}, f32[256]{0:T(256)}, u32[]{:S(2)}) copy-start(f32[256]{0:T(256)} %copy-done.77) | copy-start | bytes 3076
  2142.8 45.5 %copy-start.87 = (f32[256]{0:T(256)S(1)}, f32[256]{0:T(256)}, u32[]{:S(2)}) copy-start(f32[256]{0:T(256)} %param.32) | copy-start | bytes 3076
  2142.8 45.5 %copy-start.96 = (f32[256]{0:T(256)S(1)}, f32[256]{0:T(256)}, u32[]{:S(2)}) copy-start(f32[256]{0:T(256)} %param.33) | copy-start | bytes 3076
  2147.6 46.5 %copy-start.99 = (bf16[256]{0:T(256)(128)(2,1)S(1)}, bf16[256]{0:T(256)(128)(2,1)}, u32[]{:S(2)}) copy-start(bf16[256]{0:T(256)(128)(2,1)} %get-tuple-element.250) | copy-start | bytes 1540
  2147.6 46.5 %copy-start.101 = (bf16[256]{0:T(256)(128)(2,1)S(1)}, bf16[256]{0:T(256)(128)(2,1)}, u32[]{:S(2)}) copy-start(bf16[256]{0:T(256)(128)(2,1)} %get-tuple-element.318) | copy-start | bytes 1540
  2147.6 46.5 %copy-start.102 = (bf16[256]{0:T(256)(128)(2,1)S(1)}, bf16[256]{0:T(256)(128)(2,1)}, u32[]{:S(2)}) copy-start(bf16[256]{0:T(256)(128)(2,1)} %get-tuple-element.351) | copy-start | bytes 1540
  2147.6 87.7 %copy-start.105 = (f32[16]{0:T(128)S(1)}, f32[16]{0:T(128)}, u32[]{:S(2)}) copy-start(f32[16]{0:T(128)} %copy-done.104) | copy-start | bytes 196
  2147.6 89.0 %copy-start.63 = (f32[256]{0:T(256)S(1)}, f32[256]{0:T(256)}, u32[]{:S(2)}) copy-start(f32[256]{0:T(256)} %copy-done.61) | copy-start | bytes 3076
  2147.6 89.0 %copy-start.76 = (f32[256]{0:T(256)S(1)}, f32[256]{0:T(256)}, u32[]{:S(2)}) copy-start(f32[256]{0:T(256)} %copy-done.74) | copy-start | bytes 3076
  2147.7 89.0 %copy-start.82 = (f32[256]{0:T(256)S(1)}, f32[256]{0:T(256)}, u32[]{:S(2)}) copy-start(f32[256]{0:T(256)} %copy-done.81) | copy-start | bytes 3076
  2147.7 89.0 %copy-start.85 = (f32[256]{0:T(256)S(1)}, f32[256]{0:T(256)}, u32[]{:S(2)}) copy-start(f32[256]{0:T(256)} %param.42) | copy-start | bytes 3076
  2147.7 89.0 %copy-start.91 = (f32[256]{0:T(256)S(1)}, f32[256]{0:T(256)}, u32[]{:S(2)}) copy-start(f32[256]{0:T(256)} %copy-done.90) | copy-start | bytes 3076
  2236.7 18.0 copy-start.1
  (89 other events, 551.2 us)
Sparse Core Ops, SparseCore 0:
  21.6 59.4 all-gather.5
  137.7 56.7 all-gather.11
  196.8 54.2 reduce-scatter.4
  252.5 56.7 all-gather.7
  1674.1 54.3 reduce-scatter.6
  1730.5 56.7 all-gather.9
  1813.7 54.4 reduce-scatter.8
  1935.6 195.4 all-reduce.9
  2134.0 54.1 reduce-scatter.10
where the time goes:
time: 2270 us; the launch traced here: 2260 us
  matrix products  1190 us (52%)
  other arithmetic  460 us (20%)
  waiting for transfers between devices  367 us (16%)
  local copies, waits for them, and re-layouts  189 us (8%)
  blocking collectives  34.2 us (2%)
    dot_general x16, matrix products, masked_scores(): jnp.einsum('gdi,gdj->gij', q_block, key_rows, preferred_element_type=jnp....  378 us
    convert_element_type x8, other arithmetic, one_block(): grad_scores = (prob_f32 * (grad_probs - delta_row)).astype(jnp.bfloat16)  238 us
    dot_general x8, matrix products, one_block(): jnp.einsum('gdi,gdj->gij', g_block, value_rows, preferred_element_type=jn...  147 us
    dot_general x8, matrix products, one_block(): jnp.einsum('gdi,gij->gdj', g_block, probs_low, preferred_element_type=jnp...  134 us
    dot_general x18, matrix products, conv_input_grad(): jnp.einsum('oc,oip->cip', cols_part, moved_grads[kernel_tap], preferred_e...  131 us
    reduce_sum x8, other arithmetic, one_block(): row_total = jnp.sum(raised, axis=-1, keepdims=True)  130 us
    dot_general x8, matrix products, one_block(): jnp.einsum('gdj,gij->gdi', value_rows, probs_low, preferred_element_type=...  128 us
    psum x1, waiting for transfers between devices, local(): lax.psum(conv1_weight_grad.astype(jnp.bfloat16), 'dp').astype(jnp.float32)  119 us
  transfers between devices with their start and end apart: 9, of which 7 were waited for; matrix products, arithmetic and copies ran while one was open for 13% of the time, Pallas kernels for 0%

commit v1 on v0

--- a/solution.py
+++ b/solution.py
@@ -11,6 +11,23 @@
 CTX = 260
 EPSILON = 1e-05
 NEG_FILL = -1e30
+
+
+def in_order(blocks, dim):
+    lengths = list(blocks.shape[1:])
+    lengths[dim] *= blocks.shape[0]
+    return jnp.moveaxis(blocks, 0, dim).reshape(lengths)
+
+
+def collected_by_bits(shard, axis):
+    length, mine = (lax.axis_size(axis), lax.axis_index(axis))
+    tiles, bit = (shard[None], 1)
+    while bit < length:
+        other = lax.ppermute(tiles, axis, [(i, i ^ bit) for i in range(length)])
+        low = mine & bit == 0
+        tiles = jnp.concatenate([jnp.where(low, tiles, other), jnp.where(low, other, tiles)])
+        bit *= 2
+    return tiles
 
 
 def group_norm(values, gain_vec, bias_vec):
@@ -208,7 +225,7 @@
         + emb_bias[:, :, None]
     )
     act_two = second_section(conv_one, norm2_gain, norm2_bias, scale_shift).astype(jnp.bfloat16)
-    full_two = lax.all_gather(act_two, "tensor", axis=0, tiled=True)
+    full_two = in_order(collected_by_bits(act_two, "tensor"), 0)
     hidden = feat_f32 + convolve(full_two, conv2_weight, conv2_bias)
     normed = group_norm(hidden, norm3_gain, norm3_bias).astype(jnp.bfloat16)
     full_three = lax.all_gather(normed, "tensor", axis=0, tiled=True)

time: 2270 us -> 2340 us (1.031)
  local copies, waits for them, and re-layouts: 189 us -> 232 us
  waiting for transfers between devices: 367 us -> 393 us
    ppermute x0 -> x1, waiting for transfers between devices: none -> 75.5 us  [collected_by_bits(): other = lax.ppermute(tiles, axis, [(i, i ^ bit) for i in range(length)])]
    all_gather x1 -> x0, waiting for transfers between devices: 47.4 us -> none  [local(): full_two = lax.all_gather(act_two, 'tensor', axis=0, tiled=True)]
    concatenate x0 -> x2, local copies, waits for them, and re-layouts: none -> 33.5 us  [collected_by_bits(): jnp.concatenate([jnp.where(low, tiles, other), jnp.where(low, other, tile...]
    unnamed x235 -> x239, local copies, waits for them, and re-layouts: 68.7 us -> 70.2 us
  transfers between devices with their start and end apart: 9 -> 9, of which waited for: 7 -> 7; matrix products, arithmetic and copies ran while one was open for 13% -> 15% of each run, Pallas kernels for 0% -> 0%
where the time goes in v1:
time: 2340 us; the launch traced here: 2330 us
  matrix products  1190 us (51%)
  other arithmetic  464 us (20%)
  waiting for transfers between devices  393 us (17%)
  local copies, waits for them, and re-layouts  232 us (10%)
  blocking collectives  34.2 us (1%)
    dot_general x16, matrix products, masked_scores(): jnp.einsum('gdi,gdj->gij', q_block, key_rows, preferred_element_type=jnp....  378 us
    convert_element_type x8, other arithmetic, one_block(): grad_scores = (prob_f32 * (grad_probs - delta_row)).astype(jnp.bfloat16)  238 us
    dot_general x8, matrix products, one_block(): jnp.einsum('gdi,gdj->gij', g_block, value_rows, preferred_element_type=jn...  147 us
    dot_general x8, matrix products, one_block(): jnp.einsum('gdi,gij->gdj', g_block, probs_low, preferred_element_type=jnp...  134 us
    dot_general x18, matrix products, conv_input_grad(): jnp.einsum('oc,oip->cip', cols_part, moved_grads[kernel_tap], preferred_e...  131 us
    reduce_sum x8, other arithmetic, one_block(): row_total = jnp.sum(raised, axis=-1, keepdims=True)  130 us
    dot_general x8, matrix products, one_block(): jnp.einsum('gdj,gij->gdi', value_rows, probs_low, preferred_element_type=...  128 us
    psum x1, waiting for transfers between devices, local(): lax.psum(conv1_weight_grad.astype(jnp.bfloat16), 'dp').astype(jnp.float32)  119 us
  transfers between devices with their start and end apart: 9, of which 7 were waited for; matrix products, arithmetic and copies ran while one was open for 15% of the time, Pallas kernels for 0%

profile of v1, /device:TPU:0, one launch (start us, length us, event | category | flops | bytes accessed | tf_op | source)
XLA Modules:
  0.0 2333.5 jit_solution(13242471001993665890)
XLA Ops:
  27.8 53.2 %all-gather.4.cloned.1.call-done = bf16[512,1,4096]{0,2,1:T(8,128)(2,1)} async-done(((bf16[256,1,4096]{0,2,1:T(8,128)(2,1)}), bf16[512,1,4096]{0,2,1:T(8,128)(2,1)}) %all-gather.4.cloned.1.call-update) | async-done | bytes 4194320 | tf_op jit(solution)/shard_map/all_gather | solution.py:220
  81.0 22.1 pad_slice_fusion.8
  145.5 75.5 %collective-permute-done = bf16[1,256,1,4096]{1,3,2,0:T(8,128)(2,1)} collective-permute-done((bf16[1,256,1,4096]{1,3,2,0:T(8,128)(2,1)}, bf16[1,256,1,4096]{1,3,2,0:T(8,128)(2,1)}, u32[]{:S(2)}, u32[]{:S(2)}) %collective-permute-start) | collective-permute-done | bytes 2097184 | tf_op jit(solution)/shard_map/ppermute | solution.py:26
  227.7 27.1 %copy.117 = bf16[2,256,1,4096]{1,0,3,2:T(2,128)(2,1)} copy(bf16[2,256,1,4096]{1,3,2,0:T(8,128)(2,1)S(1)} %pad_maximum_fusion.1) | data formatting | bytes 8388608 | tf_op jit(solution)/shard_map/concatenate | solution.py:28
  268.8 21.9 pad_slice_fusion
  331.6 49.8 %all-gather.6.cloned.1.call-done = bf16[512,1,4096]{0,2,1:T(8,128)(2,1)} async-done(((bf16[256,1,4096]{0,2,1:T(8,128)(2,1)}), bf16[512,1,4096]{0,2,1:T(8,128)(2,1)}) %all-gather.6.cloned.1.call-update) | async-done | bytes 4194320 | tf_op jit(solution)/shard_map/all_gather | solution.py:231
  394.9 393.9 %while.30 = (s32[]{:T(128)}, bf16[8,4,64,512]{3,2,1,0:T(8,128)(2,1)}, f32[8,4,512,1]{2,1,3,0:T(4,128)S(1)}, f32[8,4,512,1]{2,1,3,0:T(4,128)S(1)}, bf16[8,4,64,51...) while((s32[]{:T(128)}, ...), condition=%wide.region_15.16_spmd.clone, body=%wide.region_12.15_spmd.clone.sunk | while | flops 2390978560 | bytes 121079936 | solution.py:137
  444.1 16.9 fusion.445
  542.6 16.9 fusion.445
  641.1 16.9 fusion.445
  788.8 921.7 %while.31 = (s32[]{:T(128)}, f32[4,64,4356]{2,1,0:T(8,128)}, f32[4,64,4356]{2,1,0:T(8,128)}, bf16[8,4,64,512]{3,2,1,0:T(8,128)(2,1)}, bf16[8,4,64,512]{3,2,1,0:T...) while((s32[]{:T(128)}, f32[4,64,4356]{2,1,0:T(8,128)}, ...), condition=%wide.region_19.20_spmd.clone, body=%wide.region_17.19_spmd.clone.sunk | while | flops 5804411904 | bytes 302971552 | solution.py:176
  789.2 18.3 fusion.457
  807.5 30.2 %multiply_reduce_fusion.7 = (f32[4,512]{1,0:T(4,128)S(1)}, f32[4,512,4356]{1,2,0:T(8,128)}) fusion(f32[4,512,4356]{1,2,0:T(8,128)} %fusion.457, f32[4,512]{1,0:T(4,128)S(1)} %get-tuple-element.510, f32[4,512]{1,0:T(4,128)S(1)} %get-tuple-element.511, bf16[4,64,4356]{2,1,0:T(8,128)(2,1)} %get-tuple-element.572, ...), kind=kOutput, calls=%fused_computation.20.clone.1 | convolution fusion | flops 1195423744 | bytes 73890816 | tf_op jit(solution)/shard_map/while/body/eval_jaxpr/gdi,gdj->gij/dot_general | solution.py:115
  837.8 29.7 %multiply_convert_fusion.4 = bf16[4,512,4356]{1,2,0:T(8,128)(2,1)} fusion(f32[4,512,4356]{1,2,0:T(8,128)} %get-tuple-element.512, f32[4,512,4356]{1,2,0:T(8,128)} %fusion.457, f32[4,512]{1,0:T(4,128)S(1)} %get-tuple-element.513), kind=kLoop, calls=%fused_computation.19.clone.1 | loop fusion | flops 26763264 | bytes 89219072 | tf_op jit(solution)/shard_map/while/body/eval_jaxpr/convert_element_type | solution.py:163
  901.8 18.3 fusion.457
  920.1 30.2 %multiply_reduce_fusion.7 = (f32[4,512]{1,0:T(4,128)S(1)}, f32[4,512,4356]{1,2,0:T(8,128)}) fusion(f32[4,512,4356]{1,2,0:T(8,128)} %fusion.457, f32[4,512]{1,0:T(4,128)S(1)} %get-tuple-element.510, f32[4,512]{1,0:T(4,128)S(1)} %get-tuple-element.511, bf16[4,64,4356]{2,1,0:T(8,128)(2,1)} %get-tuple-element.572, ...), kind=kOutput, calls=%fused_computation.20.clone.1 | convolution fusion | flops 1195423744 | bytes 73890816 | tf_op jit(solution)/shard_map/while/body/eval_jaxpr/gdi,gdj->gij/dot_general | solution.py:115
  950.4 29.7 %multiply_convert_fusion.4 = bf16[4,512,4356]{1,2,0:T(8,128)(2,1)} fusion(f32[4,512,4356]{1,2,0:T(8,128)} %get-tuple-element.512, f32[4,512,4356]{1,2,0:T(8,128)} %fusion.457, f32[4,512]{1,0:T(4,128)S(1)} %get-tuple-element.513), kind=kLoop, calls=%fused_computation.19.clone.1 | loop fusion | flops 26763264 | bytes 89219072 | tf_op jit(solution)/shard_map/while/body/eval_jaxpr/convert_element_type | solution.py:163
  1000.3 17.0 fusion.459
  1017.3 18.3 fusion.457
  1035.6 30.3 %multiply_reduce_fusion.7 = (f32[4,512]{1,0:T(4,128)S(1)}, f32[4,512,4356]{1,2,0:T(8,128)}) fusion(f32[4,512,4356]{1,2,0:T(8,128)} %fusion.457, f32[4,512]{1,0:T(4,128)S(1)} %get-tuple-element.510, f32[4,512]{1,0:T(4,128)S(1)} %get-tuple-element.511, bf16[4,64,4356]{2,1,0:T(8,128)(2,1)} %get-tuple-element.572, ...), kind=kOutput, calls=%fused_computation.20.clone.1 | convolution fusion | flops 1195423744 | bytes 73890816 | tf_op jit(solution)/shard_map/while/body/eval_jaxpr/gdi,gdj->gij/dot_general | solution.py:115
  1065.9 29.7 %multiply_convert_fusion.4 = bf16[4,512,4356]{1,2,0:T(8,128)(2,1)} fusion(f32[4,512,4356]{1,2,0:T(8,128)} %get-tuple-element.512, f32[4,512,4356]{1,2,0:T(8,128)} %fusion.457, f32[4,512]{1,0:T(4,128)S(1)} %get-tuple-element.513), kind=kLoop, calls=%fused_computation.19.clone.1 | loop fusion | flops 26763264 | bytes 89219072 | tf_op jit(solution)/shard_map/while/body/eval_jaxpr/convert_element_type | solution.py:163
  1115.8 17.0 fusion.459
  1132.8 18.3 fusion.457
  1151.2 30.2 %multiply_reduce_fusion.7 = (f32[4,512]{1,0:T(4,128)S(1)}, f32[4,512,4356]{1,2,0:T(8,128)}) fusion(f32[4,512,4356]{1,2,0:T(8,128)} %fusion.457, f32[4,512]{1,0:T(4,128)S(1)} %get-tuple-element.510, f32[4,512]{1,0:T(4,128)S(1)} %get-tuple-element.511, bf16[4,64,4356]{2,1,0:T(8,128)(2,1)} %get-tuple-element.572, ...), kind=kOutput, calls=%fused_computation.20.clone.1 | convolution fusion | flops 1195423744 | bytes 73890816 | tf_op jit(solution)/shard_map/while/body/eval_jaxpr/gdi,gdj->gij/dot_general | solution.py:115
  1181.4 29.7 %multiply_convert_fusion.4 = bf16[4,512,4356]{1,2,0:T(8,128)(2,1)} fusion(f32[4,512,4356]{1,2,0:T(8,128)} %get-tuple-element.512, f32[4,512,4356]{1,2,0:T(8,128)} %fusion.457, f32[4,512]{1,0:T(4,128)S(1)} %get-tuple-element.513), kind=kLoop, calls=%fused_computation.19.clone.1 | loop fusion | flops 26763264 | bytes 89219072 | tf_op jit(solution)/shard_map/while/body/eval_jaxpr/convert_element_type | solution.py:163
  1231.3 17.0 fusion.459
  1248.3 18.3 fusion.457
  1266.7 30.3 %multiply_reduce_fusion.7 = (f32[4,512]{1,0:T(4,128)S(1)}, f32[4,512,4356]{1,2,0:T(8,128)}) fusion(f32[4,512,4356]{1,2,0:T(8,128)} %fusion.457, f32[4,512]{1,0:T(4,128)S(1)} %get-tuple-element.510, f32[4,512]{1,0:T(4,128)S(1)} %get-tuple-element.511, bf16[4,64,4356]{2,1,0:T(8,128)(2,1)} %get-tuple-element.572, ...), kind=kOutput, calls=%fused_computation.20.clone.1 | convolution fusion | flops 1195423744 | bytes 73890816 | tf_op jit(solution)/shard_map/while/body/eval_jaxpr/gdi,gdj->gij/dot_general | solution.py:115
  1296.9 29.7 %multiply_convert_fusion.4 = bf16[4,512,4356]{1,2,0:T(8,128)(2,1)} fusion(f32[4,512,4356]{1,2,0:T(8,128)} %get-tuple-element.512, f32[4,512,4356]{1,2,0:T(8,128)} %fusion.457, f32[4,512]{1,0:T(4,128)S(1)} %get-tuple-element.513), kind=kLoop, calls=%fused_computation.19.clone.1 | loop fusion | flops 26763264 | bytes 89219072 | tf_op jit(solution)/shard_map/while/body/eval_jaxpr/convert_element_type | solution.py:163
  1346.8 17.0 fusion.459
  1363.8 18.3 fusion.457
  1382.2 30.2 %multiply_reduce_fusion.7 = (f32[4,512]{1,0:T(4,128)S(1)}, f32[4,512,4356]{1,2,0:T(8,128)}) fusion(f32[4,512,4356]{1,2,0:T(8,128)} %fusion.457, f32[4,512]{1,0:T(4,128)S(1)} %get-tuple-element.510, f32[4,512]{1,0:T(4,128)S(1)} %get-tuple-element.511, bf16[4,64,4356]{2,1,0:T(8,128)(2,1)} %get-tuple-element.572, ...), kind=kOutput, calls=%fused_computation.20.clone.1 | convolution fusion | flops 1195423744 | bytes 73890816 | tf_op jit(solution)/shard_map/while/body/eval_jaxpr/gdi,gdj->gij/dot_general | solution.py:115
  1412.4 29.7 %multiply_convert_fusion.4 = bf16[4,512,4356]{1,2,0:T(8,128)(2,1)} fusion(f32[4,512,4356]{1,2,0:T(8,128)} %get-tuple-element.512, f32[4,512,4356]{1,2,0:T(8,128)} %fusion.457, f32[4,512]{1,0:T(4,128)S(1)} %get-tuple-element.513), kind=kLoop, calls=%fused_computation.19.clone.1 | loop fusion | flops 26763264 | bytes 89219072 | tf_op jit(solution)/shard_map/while/body/eval_jaxpr/convert_element_type | solution.py:163
  1462.4 17.0 fusion.459
  1479.4 18.3 fusion.457
  1497.7 30.2 %multiply_reduce_fusion.7 = (f32[4,512]{1,0:T(4,128)S(1)}, f32[4,512,4356]{1,2,0:T(8,128)}) fusion(f32[4,512,4356]{1,2,0:T(8,128)} %fusion.457, f32[4,512]{1,0:T(4,128)S(1)} %get-tuple-element.510, f32[4,512]{1,0:T(4,128)S(1)} %get-tuple-element.511, bf16[4,64,4356]{2,1,0:T(8,128)(2,1)} %get-tuple-element.572, ...), kind=kOutput, calls=%fused_computation.20.clone.1 | convolution fusion | flops 1195423744 | bytes 73890816 | tf_op jit(solution)/shard_map/while/body/eval_jaxpr/gdi,gdj->gij/dot_general | solution.py:115
  1528.0 29.7 %multiply_convert_fusion.4 = bf16[4,512,4356]{1,2,0:T(8,128)(2,1)} fusion(f32[4,512,4356]{1,2,0:T(8,128)} %get-tuple-element.512, f32[4,512,4356]{1,2,0:T(8,128)} %fusion.457, f32[4,512]{1,0:T(4,128)S(1)} %get-tuple-element.513), kind=kLoop, calls=%fused_computation.19.clone.1 | loop fusion | flops 26763264 | bytes 89219072 | tf_op jit(solution)/shard_map/while/body/eval_jaxpr/convert_element_type | solution.py:163
  1577.8 17.0 fusion.459
  1594.8 18.3 fusion.457
  1613.2 30.2 %multiply_reduce_fusion.7 = (f32[4,512]{1,0:T(4,128)S(1)}, f32[4,512,4356]{1,2,0:T(8,128)}) fusion(f32[4,512,4356]{1,2,0:T(8,128)} %fusion.457, f32[4,512]{1,0:T(4,128)S(1)} %get-tuple-element.510, f32[4,512]{1,0:T(4,128)S(1)} %get-tuple-element.511, bf16[4,64,4356]{2,1,0:T(8,128)(2,1)} %get-tuple-element.572, ...), kind=kOutput, calls=%fused_computation.20.clone.1 | convolution fusion | flops 1195423744 | bytes 73890816 | tf_op jit(solution)/shard_map/while/body/eval_jaxpr/gdi,gdj->gij/dot_general | solution.py:115
  1643.4 29.7 %multiply_convert_fusion.4 = bf16[4,512,4356]{1,2,0:T(8,128)(2,1)} fusion(f32[4,512,4356]{1,2,0:T(8,128)} %get-tuple-element.512, f32[4,512,4356]{1,2,0:T(8,128)} %fusion.457, f32[4,512]{1,0:T(4,128)S(1)} %get-tuple-element.513), kind=kLoop, calls=%fused_computation.19.clone.1 | loop fusion | flops 26763264 | bytes 89219072 | tf_op jit(solution)/shard_map/while/body/eval_jaxpr/convert_element_type | solution.py:163
  1693.3 17.0 fusion.459
  1755.0 45.2 %reduce-scatter.7.cloned.1.call-done = bf16[256,1,4096]{0,2,1:T(8,128)(2,1)} async-done(((bf16[512,1,4096]{0,2,1:T(8,128)(2,1)}), bf16[256,1,4096]{0,2,1:T(8,128)(2,1)}) %reduce-scatter.7.cloned.1.call-update) | async-done | bytes 2097168 | tf_op jit(solution)/shard_map/reduce_scatter | solution.py:293
  1861.2 24.3 %fusion.43 = bf16[512,1,4096]{0,2,1:T(8,128)(2,1)} fusion(bf16[256,4096]{0,1:T(8,128)(2,1)} %bitcast.796, f32[4096,512]{1,0:T(8,128)} %fusion.339, f32[4096,512]{1,0:T(8,128)} %fusion.338, f32[4096,512]{1,0:T(8,128)} %fusion.337, f32[4096,512]{1,0:T(8,128)} %fusion.133, f32[4096,512]{1,0:T(8,128)} %fusion.336, f32[4096,512]{1,0:T(8,128)} %fusion.335, ...), kind=kOutput, calls=%fused_computation.63 | convolution fusion | flops 1092616192 | bytes 73662464 | tf_op jit(solution)/shard_map/oc,oip->cip/dot_general | solution.py:87
  2037.5 25.3 %fusion.44 = bf16[512,1,4096]{0,2,1:T(8,128)(2,1)} fusion(bf16[256,4096]{0,1:T(8,128)(2,1)} %bitcast.795, f32[4096,512]{1,0:T(8,128)} %fusion.332, f32[4096,512]{1,0:T(8,128)} %fusion.331, f32[4096,512]{1,0:T(8,128)} %fusion.330, f32[4096,512]{1,0:T(8,128)} %fusion.113, f32[4096,512]{1,0:T(8,128)} %fusion.329, f32[4096,512]{1,0:T(8,128)} %fusion.328, ...), kind=kOutput, calls=%fused_computation.64 | convolution fusion | flops 1092616192 | bytes 73662464 | tf_op jit(solution)/shard_map/oc,oip->cip/dot_general | solution.py:87
  2083.8 119.0 %all-reduce.10.cloned.1.call-done = (bf16[256,4608]{0,1:T(8,128)(2,1)}, bf16[256,4608]{0,1:T(8,128)(2,1)}, bf16[256,512]{0,1:T(8,128)(2,1)}, bf16[2,2048,256]{2,...) async-done(((bf16[256,4608]{0,1:T(8,128)(2,1)}, bf16[256,4608]{0,1:T(8,128)(2,1)}, bf16[256,512]{0,1:T(8,128)(2,1)}, ...) | async-done | bytes 9961488 | tf_op jit(solution)/shard_map/psum | solution.py:335
  2219.4 40.5 %reduce-scatter.11.cloned.1.call-done = bf16[256,1,4096]{0,2,1:T(8,128)(2,1)} async-done(((bf16[512,1,4096]{0,2,1:T(8,128)(2,1)}), bf16[256,1,4096]{0,2,1:T(8,128)(2,1)}) %reduce-scatter.11.cloned.1.call-update) | async-done | bytes 2097168 | tf_op jit(solution)/shard_map/reduce_scatter | solution.py:90
  2265.8 34.2 %all-reduce.6 = (bf16[256]{0:T(256)(128)(2,1)S(1)}, bf16[256]{0:T(256)(128)(2,1)S(1)}, bf16[256]{0:T(256)(128)(2,1)S(1)}, bf16[2,256]{1,0:T(2,128)(2,1)S(1)}, bf...) all-reduce(bf16[256]{0:T(256)(128)(2,1)S(1)} %get-tuple-element.252, ...), channel_id=1, replica_groups=mesh['dp'=16,'tensor'=2] {'dp'}, use_global_device_ids=true, to_apply=%region_42.43 | all-reduce | flops 4096 | bytes 16384 | tf_op jit(solution)/shard_map/psum | solution.py:333
  (547 shorter events, 981.8 us)
Async XLA Ops:
  7.2 317.5 %copy-start = (bf16[2,256,2048]{2,1,0:T(8,128)(2,1)S(1)}, bf16[2,256,2048]{2,1,0:T(8,128)(2,1)}, u32[]{:S(2)}) copy-start(bf16[2,256,2048]{2,1,0:T(8,128)(2,1)} %param.46) | copy-start | bytes 6291460
  7.2 73.8 %all-gather.4.cloned.1.call-start = ((), (), s32[]{:S(2)}) async-start(), calls=%async_computation.4 | async-start | bytes 6291456 | tf_op jit(solution)/shard_map/all_gather | solution.py:220
  21.5 306.4 %reduce-scatter.5.cloned.1.call-start = ((), (), s32[]{:S(2)}) async-start(), calls=%async_computation.7 | async-start | bytes 6291456 | tf_op jit(solution)/shard_map/reduce_scatter | solution.py:263
  27.8 193.3 %copy-start.72 = (f32[1,256]{1,0:T(1,128)}, f32[1,256]{1,0:T(1,128)S(1)}, u32[]{:S(2)}) copy-start(f32[1,256]{1,0:T(1,128)S(1)} %get-tuple-element.372) | copy-start | bytes 3076
  27.8 193.3 %copy-start.85 = (f32[1,256]{1,0:T(1,128)}, f32[1,256]{1,0:T(1,128)S(1)}, u32[]{:S(2)}) copy-start(f32[1,256]{1,0:T(1,128)S(1)} %get-tuple-element.373) | copy-start | bytes 3076
  81.0 22.1 copy-start.99
  103.1 17.8 copy-start.18
  103.1 19.1 copy-start.16
  103.1 20.5 copy-start.14
  103.1 21.8 copy-start.12
  128.5 92.6 %copy-start.66 = (f32[256]{0:T(256)}, f32[256]{0:T(256)S(1)}, u32[]{:S(2)}) copy-start(f32[256]{0:T(256)S(1)} %sub.167) | copy-start | bytes 3076
  132.2 88.9 %copy-start.70 = (f32[256]{0:T(256)}, f32[256]{0:T(256)S(1)}, u32[]{:S(2)}) copy-start(f32[256]{0:T(256)S(1)} %mul.411) | copy-start | bytes 3076
  137.6 83.5 %collective-permute-start = (bf16[1,256,1,4096]{1,3,2,0:T(8,128)(2,1)}, bf16[1,256,1,4096]{1,3,2,0:T(8,128)(2,1)}, u32[]{:S(2)}, u32[]{:S(2)}) collective-permute-start(bf16[1,256,1,4096]{1,3,2,0:T(8,128)(2,1)} %fusion.137), channel_id=1, source_target_pairs={{0,1},{1,0},{2,3},{3,2},{4,5},{5,4},{6,7},{7,6},{8,9},{9,8},{10,11... | collective-permute-start | bytes 6291464 | tf_op jit(solution)/shard_map/ppermute | solution.py:26
  141.2 240.2 %all-gather.6.cloned.1.call-start = ((), (), s32[]{:S(2)}) async-start(), calls=%async_computation.5 | async-start | bytes 6291456 | tf_op jit(solution)/shard_map/all_gather | solution.py:231
  268.8 22.0 copy-start.100
  290.7 17.8 copy-start.30
  290.7 19.2 copy-start.28
  290.7 20.5 copy-start.26
  290.8 21.8 copy-start.8
  324.6 1475.7 %reduce-scatter.7.cloned.1.call-start = ((), (), s32[]{:S(2)}) async-start(), calls=%async_computation.8 | async-start | bytes 6291456 | tf_op jit(solution)/shard_map/reduce_scatter | solution.py:293
  324.7 56.7 %copy-start.112 = (bf16[3,256,512]{2,1,0:T(8,128)(2,1)S(1)}, bf16[3,256,512]{2,1,0:T(8,128)(2,1)}, u32[]{:S(2)}) copy-start(bf16[3,256,512]{2,1,0:T(8,128)(2,1)} %param.44) | copy-start | bytes 2359300
  324.7 56.7 %copy-start.114 = (f32[3,256]{1,0:T(4,128)S(1)}, f32[3,256]{1,0:T(4,128)}, u32[]{:S(2)}) copy-start(f32[3,256]{1,0:T(4,128)} %param.45) | copy-start | bytes 9220
  461.1 16.3 copy-start.6
  510.3 16.3 copy-start.6
  1745.8 155.0 %all-gather.8.cloned.1.call-start = ((), (), s32[]{:S(2)}) async-start(), calls=%async_computation.6 | async-start | bytes 6291456 | tf_op jit(solution)/shard_map/all_gather | solution.py:251
  1752.6 47.7 %copy-start.64 = (f32[256]{0:T(256)S(1)}, f32[256]{0:T(256)}, u32[]{:S(2)}) copy-start(f32[256]{0:T(256)} %copy-done.63) | copy-start | bytes 3076
  1752.6 47.7 %copy-start.77 = (f32[256]{0:T(256)S(1)}, f32[256]{0:T(256)}, u32[]{:S(2)}) copy-start(f32[256]{0:T(256)} %copy-done.76) | copy-start | bytes 3076
  1752.6 47.7 %copy-start.88 = (f32[256]{0:T(256)S(1)}, f32[256]{0:T(256)}, u32[]{:S(2)}) copy-start(f32[256]{0:T(256)} %param.42) | copy-start | bytes 3076
  1755.0 50.2 %copy-start.111 = (f32[16]{0:T(128)S(1)}, f32[16]{0:T(128)}, u32[]{:S(2)}) copy-start(f32[16]{0:T(128)} %copy-done.110) | copy-start | bytes 196
  1755.0 185.2 %reduce-scatter.9.cloned.1.call-start = ((), (), s32[]{:S(2)}) async-start(), calls=%async_computation.9 | async-start | bytes 6291456 | tf_op jit(solution)/shard_map/reduce_scatter | solution.py:90
  1885.6 317.2 %all-reduce.10.cloned.1.call-start = ((), (), s32[]{:S(2)}) async-start(), calls=%async_computation.11 | async-start | bytes 19922944 | tf_op jit(solution)/shard_map/psum | solution.py:335
  1930.8 16.9 copy-start.109
  2007.2 252.7 %reduce-scatter.11.cloned.1.call-start = ((), (), s32[]{:S(2)}) async-start(), calls=%async_computation.10 | async-start | bytes 6291456 | tf_op jit(solution)/shard_map/reduce_scatter | solution.py:90
  2214.4 45.5 %copy-start.5 = (bf16[256,1,4096]{0,2,1:T(8,128)(2,1)S(1)}, bf16[256,1,4096]{0,2,1:T(8,128)(2,1)}, u32[]{:S(2)}) copy-start(bf16[256,1,4096]{0,2,1:T(8,128)(2,1)} %copy.106) | copy-start | bytes 6291460
  2214.4 45.5 %copy-start.69 = (f32[256]{0:T(256)S(1)}, f32[256]{0:T(256)}, u32[]{:S(2)}) copy-start(f32[256]{0:T(256)} %copy-done.68) | copy-start | bytes 3076
  2214.4 45.5 %copy-start.82 = (f32[256]{0:T(256)S(1)}, f32[256]{0:T(256)}, u32[]{:S(2)}) copy-start(f32[256]{0:T(256)} %copy-done.81) | copy-start | bytes 3076
  2214.4 45.5 %copy-start.91 = (f32[256]{0:T(256)S(1)}, f32[256]{0:T(256)}, u32[]{:S(2)}) copy-start(f32[256]{0:T(256)} %param.32) | copy-start | bytes 3076
  2214.4 45.4 %copy-start.98 = (f32[256]{0:T(256)S(1)}, f32[256]{0:T(256)}, u32[]{:S(2)}) copy-start(f32[256]{0:T(256)} %param.33) | copy-start | bytes 3076
  2219.3 46.4 %copy-start.101 = (bf16[256]{0:T(256)(128)(2,1)S(1)}, bf16[256]{0:T(256)(128)(2,1)}, u32[]{:S(2)}) copy-start(bf16[256]{0:T(256)(128)(2,1)} %get-tuple-element.250) | copy-start | bytes 1540
  2219.3 46.4 %copy-start.103 = (bf16[256]{0:T(256)(128)(2,1)S(1)}, bf16[256]{0:T(256)(128)(2,1)}, u32[]{:S(2)}) copy-start(bf16[256]{0:T(256)(128)(2,1)} %get-tuple-element.318) | copy-start | bytes 1540
  2219.3 46.4 %copy-start.104 = (bf16[256]{0:T(256)(128)(2,1)S(1)}, bf16[256]{0:T(256)(128)(2,1)}, u32[]{:S(2)}) copy-start(bf16[256]{0:T(256)(128)(2,1)} %get-tuple-element.353) | copy-start | bytes 1540
  2219.3 87.7 %copy-start.107 = (f32[16]{0:T(128)S(1)}, f32[16]{0:T(128)}, u32[]{:S(2)}) copy-start(f32[16]{0:T(128)} %copy-done.106) | copy-start | bytes 196
  2219.3 89.0 %copy-start.65 = (f32[256]{0:T(256)S(1)}, f32[256]{0:T(256)}, u32[]{:S(2)}) copy-start(f32[256]{0:T(256)} %copy-done.63) | copy-start | bytes 3076
  2219.3 89.0 %copy-start.78 = (f32[256]{0:T(256)S(1)}, f32[256]{0:T(256)}, u32[]{:S(2)}) copy-start(f32[256]{0:T(256)} %copy-done.76) | copy-start | bytes 3076
  2219.3 89.0 %copy-start.84 = (f32[256]{0:T(256)S(1)}, f32[256]{0:T(256)}, u32[]{:S(2)}) copy-start(f32[256]{0:T(256)} %copy-done.83) | copy-start | bytes 3076
  2219.3 89.0 %copy-start.89 = (f32[256]{0:T(256)S(1)}, f32[256]{0:T(256)}, u32[]{:S(2)}) copy-start(f32[256]{0:T(256)} %param.42) | copy-start | bytes 3076
  2219.4 89.0 %copy-start.95 = (f32[256]{0:T(256)S(1)}, f32[256]{0:T(256)}, u32[]{:S(2)}) copy-start(f32[256]{0:T(256)} %copy-done.94) | copy-start | bytes 3076
  2308.4 18.0 copy-start.1
  (91 other events, 578.2 us)
Sparse Core Ops, SparseCore 0:
  21.6 59.4 all-gather.3
  141.3 90.1 reduce-scatter.4
  324.7 56.7 all-gather.5
  1745.9 54.3 reduce-scatter.6
  1802.2 56.7 all-gather.7
  1885.7 54.4 reduce-scatter.8
  2007.3 195.4 all-reduce.9
  2205.7 54.1 reduce-scatter.10
